TPU v7x, 32 devices: a whole 2x2x4 slice. The times are simulated.
32 devices in a mesh: coef: 16 (over z, y, x), rot: 2 (over core).
Axes of the slice: x: 2, y: 2, z: 4, core: 2. Of those that a mesh axis runs over, the one named last changes fastest.
Arguments:
- features: float32 [256, 47872], P(None, 'coef'), may hold values from -200 to 200
- table: float32 [2048, 47872], P('rot', 'coef'), may hold values from -16 to 16
- targets: float32 [256, 2048], P('coef', 'rot'), may hold values from 0 to 1
Outputs:
- grad_features: float32 [256, 47872], P('rot', 'coef')
- grad_table: float32 [2048, 47872], P('rot', 'coef')
All inputs are finite; a program needn't handle non-finite values.
Results may differ from a plain program's by a relative error of at most 0.0003.
Values sent between devices are 32-bit elements; how exact they have to be, the bound alone decides.
No kernel may reach another device: no remote copies, remote signals or barrier semaphores. Data moves between devices by JAX's collectives and lax.ppermute only.
A program may use at most 64 MiB of HBM per device.

v0:
```python
import math
import jax
import jax.numpy as jnp
from jax import lax
from jax.sharding import PartitionSpec as P

K = 47872
logit_gain = 4.0
loss_scale = 64.0


def on_device(features, table, targets):
    scale = logit_gain / math.sqrt(K)
    partial_value = lax.dot_general(
        features,
        table,
        (((1,), (1,)), ((), ())),
        precision=lax.Precision.HIGHEST,
        preferred_element_type=jnp.float32,
    )
    summed = lax.psum_scatter(partial_value, "coef", scatter_dimension=0, tiled=True)
    scores = scale * summed
    local_max = jnp.max(scores, axis=1)
    row_max = lax.pmax(local_max, "rot")
    expo = jnp.exp(scores - row_max[:, None])
    row_total = lax.psum(jnp.sum(expo, axis=1), "rot")
    probs = expo / row_total[:, None]
    grad_scores = loss_scale * (probs - targets)
    piece = lax.all_gather(grad_scores, "coef", axis=0, tiled=True)
    table_part = lax.dot_general(
        piece,
        features,
        (((0,), (0,)), ((), ())),
        precision=lax.Precision.HIGHEST,
        preferred_element_type=jnp.float32,
    )
    feature_part = jnp.dot(
        piece, table, precision=lax.Precision.HIGHEST, preferred_element_type=jnp.float32
    )
    grad_features = scale * lax.psum_scatter(feature_part, "rot", scatter_dimension=0, tiled=True)
    grad_table = scale * table_part
    return (grad_features, grad_table)


def solution(mesh):
    return jax.shard_map(
        on_device,
        mesh=mesh,
        in_specs=(P(None, "coef"), P("rot", "coef"), P("coef", "rot")),
        out_specs=(P("rot", "coef"), P("rot", "coef")),
        check_vma=False,
    )
```

profile of v0, /device:TPU:0, one launch (start us, length us, event | category | flops | bytes accessed | tf_op | source)
XLA Modules:
  0.0 202.1 jit_solution(17302437431089537872)
XLA Ops:
  7.2 0.0 copy-start
  7.2 0.0 copy-start.1
  7.2 0.0 reduce-scatter.3.cloned.1.call-start
  7.2 1.8 copy-done
  9.0 14.6 %fusion.1 = f32[256,1024]{1,0:T(8,128)} fusion(f32[256,2992]{0,1:T(8,128)S(1)} %copy-done, f32[1024,2992]{0,1:T(8,128)} %param.4), kind=kOutput, calls=%fused_computation.6 | convolution fusion | flops 9412018176 | bytes 16367616 | tf_op jit(solution)/shard_map/dot_general | solution.py:14
  23.6 0.0 reduce-scatter.3.cloned.1.call-update
  23.7 0.0 all-gather.2.cloned.1.call-start
  23.7 81.6 %reduce-scatter.3.cloned.1.call-done = f32[16,1024]{1,0:T(8,128)} async-done(((f32[256,1024]{1,0:T(8,128)}), f32[16,1024]{1,0:T(8,128)}) %reduce-scatter.3.cloned.1.call-update) | async-done | bytes 65552 | tf_op jit(solution)/shard_map/reduce_scatter | solution.py:21
  105.3 1.0 multiply_reduce_fusion
  106.3 2.5 %pmax.7 = f32[16]{0:T(128)S(1)} all-reduce(f32[16]{0:T(128)S(1)} %multiply_reduce_fusion), channel_id=1, replica_groups=mesh['coef'=16,'rot'=2] {'rot'}, use_global_device_ids=true, to_apply=%region_2.0 | all-reduce | flops 16 | bytes 128 | tf_op jit(solution)/shard_map/pmax | solution.py:24
  108.8 1.0 fusion
  109.8 2.5 %psum.7 = f32[16]{0:T(128)S(1)} all-reduce(f32[16]{0:T(128)S(1)} %fusion), channel_id=1, replica_groups=mesh['coef'=16,'rot'=2] {'rot'}, use_global_device_ids=true, to_apply=%region_4.0 | all-reduce | flops 16 | bytes 128 | tf_op jit(solution)/shard_map/psum | solution.py:26
  112.3 0.0 copy-done.1
  112.3 1.6 subtract_multiply_fusion
  113.8 0.0 all-gather.2.cloned.1.call-update
  113.8 0.2 reduce-scatter.5.cloned.1.call-start
  114.1 51.3 %all-gather.2.cloned.1.call-done = f32[256,1024]{1,0:T(8,128)} async-done(((f32[16,1024]{1,0:T(8,128)}), f32[256,1024]{1,0:T(8,128)}) %all-gather.2.cloned.1.call-update) | async-done | bytes 1048592 | tf_op jit(solution)/shard_map/all_gather | solution.py:29
  165.4 13.5 %fusion.2 = f32[256,2992]{0,1:T(8,128)} fusion(f32[256,1024]{1,0:T(8,128)} %all-gather.2.cloned.1.call-done, f32[1024,2992]{0,1:T(8,128)} %param.4), kind=kOutput, calls=%fused_computation.7 | convolution fusion | flops 9412018176 | bytes 16367616 | tf_op jit(solution)/shard_map/dot_general | solution.py:37
  178.9 0.0 reduce-scatter.5.cloned.1.call-update
  178.9 14.0 %convolution_multiply_fusion = f32[1024,2992]{0,1:T(8,128)} fusion(f32[256,1024]{1,0:T(8,128)} %all-gather.2.cloned.1.call-done, f32[256,2992]{0,1:T(8,128)S(1)} %copy-done), kind=kOutput, calls=%fused_computation | convolution fusion | flops 9415081984 | bytes 16367616 | tf_op jit(solution)/shard_map/dot_general | solution.py:30
  192.9 0.0 reduce-scatter.5.cloned.1.call-done
  192.9 2.7 %broadcast_multiply_fusion = f32[128,2992]{0,1:T(8,128)} fusion(f32[128,2992]{0,1:T(8,128)} %reduce-scatter.5.cloned.1.call-done), kind=kLoop, calls=%fused_computation.1 | loop fusion | flops 382976 | bytes 3063808 | tf_op jit(solution)/shard_map/mul | solution.py:40
Async XLA Ops:
  7.2 1.9 copy-start
  7.2 105.1 %copy-start.1 = (f32[16,1024]{1,0:T(8,128)S(1)}, f32[16,1024]{1,0:T(8,128)}, u32[]{:S(2)}) copy-start(f32[16,1024]{1,0:T(8,128)} %param.5) | copy-start | bytes 196612
  7.2 98.1 %reduce-scatter.3.cloned.1.call-start = ((), (), s32[]{:S(2)}) async-start(), calls=%async_computation.2 | async-start | bytes 1114112 | tf_op jit(solution)/shard_map/reduce_scatter | solution.py:21
  23.7 141.8 %all-gather.2.cloned.1.call-start = ((), (), s32[]{:S(2)}) async-start(), calls=%async_computation.3 | async-start | bytes 1114112 | tf_op jit(solution)/shard_map/all_gather | solution.py:29
  113.8 79.1 %reduce-scatter.5.cloned.1.call-start = ((), (), s32[]{:S(2)}) async-start(), calls=%async_computation.4 | async-start | bytes 4595712 | tf_op jit(solution)/shard_map/reduce_scatter | solution.py:40
Sparse Core Ops, SparseCore 0:
  23.8 81.4 reduce-scatter.2
  114.0 51.4 all-gather.1
  179.0 9.6 reduce-scatter.4
where the time goes:
time: 202 us
  waiting for transfers between devices  133 us (66%)
  matrix products  42.1 us (21%)
  between operations  13.8 us (7%)
  other arithmetic  6.2 us (3%)
  blocking collectives  4.93 us (2%)
    reduce_scatter x1, waiting for transfers between devices, on_device(): lax.psum_scatter(partial_value, 'coef', scatter_dimension=0, tiled=True)  81.6 us
    all_gather x1, waiting for transfers between devices, on_device(): piece = lax.all_gather(grad_scores, 'coef', axis=0, tiled=True)  51.3 us
    dot_general x1, matrix products, on_device(): lax.dot_general(features, table, (((1,), (1,)), ((), ())), precision=lax....  14.6 us
    dot_general x1, matrix products, on_device(): lax.dot_general(piece, features, (((0,), (0,)), ((), ())), precision=lax....  14 us
    dot_general x1, matrix products, on_device(): jnp.dot(piece, table, precision=lax.Precision.HIGHEST, preferred_element_...  13.5 us
  transfers between devices with their start and end apart: 3, of which 2 were waited for; matrix products, arithmetic and copies ran while one was open for 7% of the time, Pallas kernels for 0%

commit v1 on v0

--- a/solution.py
+++ b/solution.py
@@ -26,7 +26,12 @@
     row_total = lax.psum(jnp.sum(expo, axis=1), "rot")
     probs = expo / row_total[:, None]
     grad_scores = loss_scale * (probs - targets)
-    piece = lax.all_gather(grad_scores, "coef", axis=0, tiled=True)
+    ring = [grad_scores]
+    for hop in range(15):
+        ring.append(lax.ppermute(ring[-1], "coef", [(dev, (dev + 1) % 16) for dev in range(16)]))
+    piece = jnp.roll(
+        jnp.concatenate(ring[::-1], axis=0), (lax.axis_index("coef") + 1) * ring[0].shape[0], axis=0
+    )
     table_part = lax.dot_general(
         piece,
         features,

time: 202 us -> 287 us (1.42)
  waiting for transfers between devices: 133 us -> 201 us
  local copies, waits for them, and re-layouts: 1.81 us -> 17 us
    ppermute x0 -> x15, waiting for transfers between devices: none -> 120 us  [on_device(): lax.ppermute(ring[-1], 'coef', [(dev, (dev + 1) % 16) for dev in range(16)])]
    all_gather x1 -> x0, waiting for transfers between devices: 51.3 us -> none  [on_device(): piece = lax.all_gather(grad_scores, 'coef', axis=0, tiled=True)]
    unnamed x4 -> x65, local copies, waits for them, and re-layouts: 1.81 us -> 17 us
  transfers between devices with their start and end apart: 3 -> 17, of which waited for: 2 -> 16; matrix products, arithmetic and copies ran while one was open for 7% -> 5% of each run, Pallas kernels for 0% -> 0%
where the time goes in v1:
time: 287 us; the launch traced here: 286 us
  waiting for transfers between devices  201 us (70%)
  matrix products  42.8 us (15%)
  local copies, waits for them, and re-layouts  17 us (6%)
  between operations  14.4 us (5%)
  other arithmetic  5.58 us (2%)
  blocking collectives  4.93 us (2%)
    ppermute x15, waiting for transfers between devices, on_device(): lax.ppermute(ring[-1], 'coef', [(dev, (dev + 1) % 16) for dev in range(16)])  120 us
    reduce_scatter x1, waiting for transfers between devices, on_device(): lax.psum_scatter(partial_value, 'coef', scatter_dimension=0, tiled=True)  81.6 us
    unnamed x65, local copies, waits for them, and re-layouts  17 us
    dot_general x1, matrix products, on_device(): lax.dot_general(features, table, (((1,), (1,)), ((), ())), precision=lax....  14.6 us
    dot_general x1, matrix products, on_device(): jnp.dot(piece, table, precision=lax.Precision.HIGHEST, preferred_element_...  14.2 us
    dot_general x1, matrix products, on_device(): lax.dot_general(piece, features, (((0,), (0,)), ((), ())), precision=lax....  14 us
  transfers between devices with their start and end apart: 17, of which 16 were waited for; matrix products, arithmetic and copies ran while one was open for 5% of the time, Pallas kernels for 0%

profile of v1, /device:TPU:0, one launch (start us, length us, event | category | flops | bytes accessed | tf_op | source)
XLA Modules:
  0.0 286.2 jit_solution(15123278184882092521)
XLA Ops:
  7.2 0.0 reduce-scatter.3.cloned.1.call-start
  7.2 1.8 copy-done
  9.0 14.6 %fusion.6 = f32[256,1024]{1,0:T(8,128)} fusion(f32[256,2992]{0,1:T(8,128)S(1)} %copy-done, f32[1024,2992]{0,1:T(8,128)} %param.4), kind=kOutput, calls=%fused_computation.43 | convolution fusion | flops 9412018176 | bytes 16367616 | tf_op jit(solution)/shard_map/dot_general | solution.py:14
  23.7 0.0 reduce-scatter.5.cloned.1.call-start
  23.7 81.6 %reduce-scatter.3.cloned.1.call-done = f32[16,1024]{1,0:T(8,128)} async-done(((f32[256,1024]{1,0:T(8,128)}), f32[16,1024]{1,0:T(8,128)}) %reduce-scatter.3.cloned.1.call-update) | async-done | bytes 65552 | tf_op jit(solution)/shard_map/reduce_scatter | solution.py:21
  105.3 1.0 multiply_reduce_fusion
  106.3 2.5 pmax.7
  108.8 1.0 fusion.3
  109.8 2.5 psum.7
  112.3 0.9 subtract_multiply_fusion
  113.2 0.1 collective-permute-start
  113.3 7.8 %collective-permute-done = f32[16,1024]{1,0:T(8,128)S(1)} collective-permute-done((f32[16,1024]{1,0:T(8,128)S(1)}, f32[16,1024]{1,0:T(8,128)S(1)}, u32[]{:S(2)}, u32[]{:S(2)}) %collective-permute-start) | collective-permute-done | bytes 65568 | tf_op jit(solution)/shard_map/ppermute | solution.py:31
  121.1 7.9 %collective-permute-done.1 = f32[16,1024]{1,0:T(8,128)S(1)} collective-permute-done((f32[16,1024]{1,0:T(8,128)S(1)}, f32[16,1024]{1,0:T(8,128)S(1)}, u32[]{:S(2)}, u32[]{:S(2)}) %collective-permute-start.1) | collective-permute-done | bytes 65568 | tf_op jit(solution)/shard_map/ppermute | solution.py:31
  129.0 7.9 %collective-permute-done.2 = f32[16,1024]{1,0:T(8,128)S(1)} collective-permute-done((f32[16,1024]{1,0:T(8,128)S(1)}, f32[16,1024]{1,0:T(8,128)S(1)}, u32[]{:S(2)}, u32[]{:S(2)}) %collective-permute-start.2) | collective-permute-done | bytes 65568 | tf_op jit(solution)/shard_map/ppermute | solution.py:31
  136.8 7.9 %collective-permute-done.3 = f32[16,1024]{1,0:T(8,128)S(1)} collective-permute-done((f32[16,1024]{1,0:T(8,128)S(1)}, f32[16,1024]{1,0:T(8,128)S(1)}, u32[]{:S(2)}, u32[]{:S(2)}) %collective-permute-start.3) | collective-permute-done | bytes 65568 | tf_op jit(solution)/shard_map/ppermute | solution.py:31
  144.7 7.9 %collective-permute-done.4 = f32[16,1024]{1,0:T(8,128)S(1)} collective-permute-done((f32[16,1024]{1,0:T(8,128)S(1)}, f32[16,1024]{1,0:T(8,128)S(1)}, u32[]{:S(2)}, u32[]{:S(2)}) %collective-permute-start.4) | collective-permute-done | bytes 65568 | tf_op jit(solution)/shard_map/ppermute | solution.py:31
  152.6 8.4 %collective-permute-done.5 = f32[16,1024]{1,0:T(8,128)S(1)} collective-permute-done((f32[16,1024]{1,0:T(8,128)S(1)}, f32[16,1024]{1,0:T(8,128)S(1)}, u32[]{:S(2)}, u32[]{:S(2)}) %collective-permute-start.5) | collective-permute-done | bytes 65568 | tf_op jit(solution)/shard_map/ppermute | solution.py:31
  161.0 8.3 %collective-permute-done.6 = f32[16,1024]{1,0:T(8,128)S(1)} collective-permute-done((f32[16,1024]{1,0:T(8,128)S(1)}, f32[16,1024]{1,0:T(8,128)S(1)}, u32[]{:S(2)}, u32[]{:S(2)}) %collective-permute-start.6) | collective-permute-done | bytes 65568 | tf_op jit(solution)/shard_map/ppermute | solution.py:31
  169.3 0.6 copy-done.2
  169.9 7.9 %collective-permute-done.7 = f32[16,1024]{1,0:T(8,128)S(1)} collective-permute-done((f32[16,1024]{1,0:T(8,128)S(1)}, f32[16,1024]{1,0:T(8,128)S(1)}, u32[]{:S(2)}, u32[]{:S(2)}) %collective-permute-start.7) | collective-permute-done | bytes 65568 | tf_op jit(solution)/shard_map/ppermute | solution.py:31
  177.7 0.6 copy-done.4
  178.4 7.9 %collective-permute-done.8 = f32[16,1024]{1,0:T(8,128)S(1)} collective-permute-done((f32[16,1024]{1,0:T(8,128)S(1)}, f32[16,1024]{1,0:T(8,128)S(1)}, u32[]{:S(2)}, u32[]{:S(2)}) %collective-permute-start.8) | collective-permute-done | bytes 65568 | tf_op jit(solution)/shard_map/ppermute | solution.py:31
  186.2 0.6 copy-done.6
  186.9 7.9 %collective-permute-done.9 = f32[16,1024]{1,0:T(8,128)S(1)} collective-permute-done((f32[16,1024]{1,0:T(8,128)S(1)}, f32[16,1024]{1,0:T(8,128)S(1)}, u32[]{:S(2)}, u32[]{:S(2)}) %collective-permute-start.9) | collective-permute-done | bytes 65568 | tf_op jit(solution)/shard_map/ppermute | solution.py:31
  194.7 0.6 copy-done.8
  195.4 7.9 %collective-permute-done.10 = f32[16,1024]{1,0:T(8,128)S(1)} collective-permute-done((f32[16,1024]{1,0:T(8,128)S(1)}, f32[16,1024]{1,0:T(8,128)S(1)}, u32[]{:S(2)}, u32[]{:S(2)}) %collective-permute-start.10) | collective-permute-done | bytes 65568 | tf_op jit(solution)/shard_map/ppermute | solution.py:31
  203.2 0.6 copy-done.10
  203.8 7.9 %collective-permute-done.11 = f32[16,1024]{1,0:T(8,128)S(1)} collective-permute-done((f32[16,1024]{1,0:T(8,128)S(1)}, f32[16,1024]{1,0:T(8,128)S(1)}, u32[]{:S(2)}, u32[]{:S(2)}) %collective-permute-start.11) | collective-permute-done | bytes 65568 | tf_op jit(solution)/shard_map/ppermute | solution.py:31
  211.7 0.6 copy-done.12
  212.3 8.4 %collective-permute-done.12 = f32[16,1024]{1,0:T(8,128)S(1)} collective-permute-done((f32[16,1024]{1,0:T(8,128)S(1)}, f32[16,1024]{1,0:T(8,128)S(1)}, u32[]{:S(2)}, u32[]{:S(2)}) %collective-permute-start.12) | collective-permute-done | bytes 65568 | tf_op jit(solution)/shard_map/ppermute | solution.py:31
  220.7 0.6 copy-done.14
  221.3 8.0 %collective-permute-done.13 = f32[16,1024]{1,0:T(8,128)} collective-permute-done((f32[16,1024]{1,0:T(8,128)S(1)}, f32[16,1024]{1,0:T(8,128)}, u32[]{:S(2)}, u32[]{:S(2)}) %collective-permute-start.13) | collective-permute-done | bytes 65568 | tf_op jit(solution)/shard_map/ppermute | solution.py:31
  229.4 8.1 %collective-permute-done.14 = f32[16,1024]{1,0:T(8,128)} collective-permute-done((f32[16,1024]{1,0:T(8,128)}, f32[16,1024]{1,0:T(8,128)}, u32[]{:S(2)}, u32[]{:S(2)}) %collective-permute-start.14) | collective-permute-done | bytes 65568 | tf_op jit(solution)/shard_map/ppermute | solution.py:31
  237.5 0.8 constant_dynamic-update-slice_fusion.31
  238.3 0.8 constant_dynamic-update-slice_fusion.30
  239.2 0.8 constant_dynamic-update-slice_fusion.29
  240.0 0.8 constant_dynamic-update-slice_fusion.28
  240.9 0.8 constant_dynamic-update-slice_fusion.27
  241.7 0.8 constant_dynamic-update-slice_fusion.26
  242.6 0.8 constant_dynamic-update-slice_fusion.25
  243.4 0.8 constant_dynamic-update-slice_fusion.24
  244.2 0.8 constant_dynamic-update-slice_fusion.23
  245.2 0.8 constant_dynamic-update-slice_fusion.15
  246.0 0.8 constant_dynamic-update-slice_fusion.14
  247.2 1.4 copy-done.1
  248.5 14.2 %fusion.1 = f32[256,2992]{0,1:T(8,128)} fusion(f32[1024,2992]{0,1:T(8,128)} %param.4, f32[512,1024]{1,0:T(8,128)S(1)} %constant_dynamic-update-slice_fusion, s32[]{:T(128)S(6)} %select_n.14), kind=kOutput, calls=%fused_computation.2 | convolution fusion | flops 9412018176 | bytes 16367620 | tf_op jit(solution)/shard_map/dot_general | solution.py:42
  262.7 14.0 %convolution_multiply_fusion = f32[1024,2992]{0,1:T(8,128)} fusion(f32[256,2992]{0,1:T(8,128)S(1)} %copy-done, f32[512,1024]{1,0:T(8,128)} %copy-done.1, s32[]{:T(128)S(6)} %select_n.14), kind=kOutput, calls=%fused_computation | convolution fusion | flops 9415081984 | bytes 16367620 | tf_op jit(solution)/shard_map/dot_general | solution.py:35
  276.7 2.7 broadcast_multiply_fusion
  (63 shorter events, 0.3 us)
Async XLA Ops:
  7.2 1.9 copy-start
  7.2 105.1 %copy-start.16 = (f32[16,1024]{1,0:T(8,128)S(1)}, f32[16,1024]{1,0:T(8,128)}, u32[]{:S(2)}) copy-start(f32[16,1024]{1,0:T(8,128)} %param.5) | copy-start | bytes 196612
  7.2 98.1 %reduce-scatter.3.cloned.1.call-start = ((), (), s32[]{:S(2)}) async-start(), calls=%async_computation.2 | async-start | bytes 1114112 | tf_op jit(solution)/shard_map/reduce_scatter | solution.py:21
  23.7 253.1 %reduce-scatter.5.cloned.1.call-start = ((), (), s32[]{:S(2)}) async-start(), calls=%async_computation.3 | async-start | bytes 4595712 | tf_op jit(solution)/shard_map/reduce_scatter | solution.py:45
  113.2 7.9 %collective-permute-start = (f32[16,1024]{1,0:T(8,128)S(1)}, f32[16,1024]{1,0:T(8,128)S(1)}, u32[]{:S(2)}, u32[]{:S(2)}) collective-permute-start(f32[16,1024]{1,0:T(8,128)S(1)} %subtract_multiply_fusion), channel_id=1, source_target_pairs={{0,2},{2,4},{4,6},{6,8},{8,10},{10,12},{12,14},{14,16},{16,18},{18... | collective-permute-start | bytes 196616 | tf_op jit(solution)/shard_map/ppermute | solution.py:31
  121.1 7.9 %collective-permute-start.1 = (f32[16,1024]{1,0:T(8,128)S(1)}, f32[16,1024]{1,0:T(8,128)S(1)}, u32[]{:S(2)}, u32[]{:S(2)}) collective-permute-start(f32[16,1024]{1,0:T(8,128)S(1)} %collective-permute-done), channel_id=1, source_target_pairs={{0,2},{2,4},{4,6},{6,8},{8,10},{10,12},{12,14},{14,16},{16,18},{18... | collective-permute-start | bytes 196616 | tf_op jit(solution)/shard_map/ppermute | solution.py:31
  129.0 7.9 %collective-permute-start.2 = (f32[16,1024]{1,0:T(8,128)S(1)}, f32[16,1024]{1,0:T(8,128)S(1)}, u32[]{:S(2)}, u32[]{:S(2)}) collective-permute-start(f32[16,1024]{1,0:T(8,128)S(1)} %collective-permute-done.1), channel_id=1, source_target_pairs={{0,2},{2,4},{4,6},{6,8},{8,10},{10,12},{12,14},{14,16},{16,18},{18... | collective-permute-start | bytes 196616 | tf_op jit(solution)/shard_map/ppermute | solution.py:31
  136.8 7.9 %collective-permute-start.3 = (f32[16,1024]{1,0:T(8,128)S(1)}, f32[16,1024]{1,0:T(8,128)S(1)}, u32[]{:S(2)}, u32[]{:S(2)}) collective-permute-start(f32[16,1024]{1,0:T(8,128)S(1)} %collective-permute-done.2), channel_id=1, source_target_pairs={{0,2},{2,4},{4,6},{6,8},{8,10},{10,12},{12,14},{14,16},{16,18},{18... | collective-permute-start | bytes 196616 | tf_op jit(solution)/shard_map/ppermute | solution.py:31
  144.7 7.9 %collective-permute-start.4 = (f32[16,1024]{1,0:T(8,128)S(1)}, f32[16,1024]{1,0:T(8,128)S(1)}, u32[]{:S(2)}, u32[]{:S(2)}) collective-permute-start(f32[16,1024]{1,0:T(8,128)S(1)} %collective-permute-done.3), channel_id=1, source_target_pairs={{0,2},{2,4},{4,6},{6,8},{8,10},{10,12},{12,14},{14,16},{16,18},{18... | collective-permute-start | bytes 196616 | tf_op jit(solution)/shard_map/ppermute | solution.py:31
  152.6 8.4 %collective-permute-start.5 = (f32[16,1024]{1,0:T(8,128)S(1)}, f32[16,1024]{1,0:T(8,128)S(1)}, u32[]{:S(2)}, u32[]{:S(2)}) collective-permute-start(f32[16,1024]{1,0:T(8,128)S(1)} %collective-permute-done.4), channel_id=1, source_target_pairs={{0,2},{2,4},{4,6},{6,8},{8,10},{10,12},{12,14},{14,16},{16,18},{18... | collective-permute-start | bytes 196616 | tf_op jit(solution)/shard_map/ppermute | solution.py:31
  160.9 8.3 %collective-permute-start.6 = (f32[16,1024]{1,0:T(8,128)S(1)}, f32[16,1024]{1,0:T(8,128)S(1)}, u32[]{:S(2)}, u32[]{:S(2)}) collective-permute-start(f32[16,1024]{1,0:T(8,128)S(1)} %collective-permute-done.5), channel_id=1, source_target_pairs={{0,2},{2,4},{4,6},{6,8},{8,10},{10,12},{12,14},{14,16},{16,18},{18... | collective-permute-start | bytes 196616 | tf_op jit(solution)/shard_map/ppermute | solution.py:31
  169.3 0.6 copy-start.2
  169.9 7.9 %collective-permute-start.7 = (f32[16,1024]{1,0:T(8,128)S(1)}, f32[16,1024]{1,0:T(8,128)S(1)}, u32[]{:S(2)}, u32[]{:S(2)}) collective-permute-start(f32[16,1024]{1,0:T(8,128)S(1)} %collective-permute-done.6), channel_id=1, source_target_pairs={{0,2},{2,4},{4,6},{6,8},{8,10},{10,12},{12,14},{14,16},{16,18},{18... | collective-permute-start | bytes 196616 | tf_op jit(solution)/shard_map/ppermute | solution.py:31
  177.7 0.6 copy-start.4
  178.4 7.9 %collective-permute-start.8 = (f32[16,1024]{1,0:T(8,128)S(1)}, f32[16,1024]{1,0:T(8,128)S(1)}, u32[]{:S(2)}, u32[]{:S(2)}) collective-permute-start(f32[16,1024]{1,0:T(8,128)S(1)} %collective-permute-done.7), channel_id=1, source_target_pairs={{0,2},{2,4},{4,6},{6,8},{8,10},{10,12},{12,14},{14,16},{16,18},{18... | collective-permute-start | bytes 196616 | tf_op jit(solution)/shard_map/ppermute | solution.py:31
  186.2 0.6 copy-start.6
  186.9 7.9 %collective-permute-start.9 = (f32[16,1024]{1,0:T(8,128)S(1)}, f32[16,1024]{1,0:T(8,128)S(1)}, u32[]{:S(2)}, u32[]{:S(2)}) collective-permute-start(f32[16,1024]{1,0:T(8,128)S(1)} %collective-permute-done.8), channel_id=1, source_target_pairs={{0,2},{2,4},{4,6},{6,8},{8,10},{10,12},{12,14},{14,16},{16,18},{18... | collective-permute-start | bytes 196616 | tf_op jit(solution)/shard_map/ppermute | solution.py:31
  194.7 0.6 copy-start.8
  195.4 7.9 %collective-permute-start.10 = (f32[16,1024]{1,0:T(8,128)S(1)}, f32[16,1024]{1,0:T(8,128)S(1)}, u32[]{:S(2)}, u32[]{:S(2)}) collective-permute-start(f32[16,1024]{1,0:T(8,128)S(1)} %collective-permute-done.9), channel_id=1, source_target_pairs={{0,2},{2,4},{4,6},{6,8},{8,10},{10,12},{12,14},{14,16},{16,18},{18... | collective-permute-start | bytes 196616 | tf_op jit(solution)/shard_map/ppermute | solution.py:31
  203.2 0.6 copy-start.10
  203.8 7.9 %collective-permute-start.11 = (f32[16,1024]{1,0:T(8,128)S(1)}, f32[16,1024]{1,0:T(8,128)S(1)}, u32[]{:S(2)}, u32[]{:S(2)}) collective-permute-start(f32[16,1024]{1,0:T(8,128)S(1)} %collective-permute-done.10), channel_id=1, source_target_pairs={{0,2},{2,4},{4,6},{6,8},{8,10},{10,12},{12,14},{14,16},{16,18},{18... | collective-permute-start | bytes 196616 | tf_op jit(solution)/shard_map/ppermute | solution.py:31
  211.7 0.6 copy-start.12
  212.3 8.4 %collective-permute-start.12 = (f32[16,1024]{1,0:T(8,128)S(1)}, f32[16,1024]{1,0:T(8,128)S(1)}, u32[]{:S(2)}, u32[]{:S(2)}) collective-permute-start(f32[16,1024]{1,0:T(8,128)S(1)} %collective-permute-done.11), channel_id=1, source_target_pairs={{0,2},{2,4},{4,6},{6,8},{8,10},{10,12},{12,14},{14,16},{16,18},{18... | collective-permute-start | bytes 196616 | tf_op jit(solution)/shard_map/ppermute | solution.py:31
  220.7 0.6 copy-start.14
  221.3 8.0 %collective-permute-start.13 = (f32[16,1024]{1,0:T(8,128)S(1)}, f32[16,1024]{1,0:T(8,128)}, u32[]{:S(2)}, u32[]{:S(2)}) collective-permute-start(f32[16,1024]{1,0:T(8,128)S(1)} %collective-permute-done.12), channel_id=1, source_target_pairs={{0,2},{2,4},{4,6},{6,8},{8,10},{10,12},{12,14},{14,16},{16,18},{18... | collective-permute-start | bytes 196616 | tf_op jit(solution)/shard_map/ppermute | solution.py:31
  229.3 8.2 %collective-permute-start.14 = (f32[16,1024]{1,0:T(8,128)}, f32[16,1024]{1,0:T(8,128)}, u32[]{:S(2)}, u32[]{:S(2)}) collective-permute-start(f32[16,1024]{1,0:T(8,128)} %collective-permute-done.13), channel_id=1, source_target_pairs={{0,2},{2,4},{4,6},{6,8},{8,10},{10,12},{12,14},{14,16},{16,18},{18... | collective-permute-start | bytes 196616 | tf_op jit(solution)/shard_map/ppermute | solution.py:31
  229.3 17.6 %copy-start.15 = (f32[16,1024]{1,0:T(8,128)S(1)}, f32[16,1024]{1,0:T(8,128)}, u32[]{:S(2)}) copy-start(f32[16,1024]{1,0:T(8,128)} %copy-done.14) | copy-start | bytes 196612
  229.3 17.6 %copy-start.13 = (f32[16,1024]{1,0:T(8,128)S(1)}, f32[16,1024]{1,0:T(8,128)}, u32[]{:S(2)}) copy-start(f32[16,1024]{1,0:T(8,128)} %copy-done.12) | copy-start | bytes 196612
  229.3 17.6 %copy-start.11 = (f32[16,1024]{1,0:T(8,128)S(1)}, f32[16,1024]{1,0:T(8,128)}, u32[]{:S(2)}) copy-start(f32[16,1024]{1,0:T(8,128)} %copy-done.10) | copy-start | bytes 196612
  229.3 17.6 %copy-start.9 = (f32[16,1024]{1,0:T(8,128)S(1)}, f32[16,1024]{1,0:T(8,128)}, u32[]{:S(2)}) copy-start(f32[16,1024]{1,0:T(8,128)} %copy-done.8) | copy-start | bytes 196612
  229.3 17.6 %copy-start.7 = (f32[16,1024]{1,0:T(8,128)S(1)}, f32[16,1024]{1,0:T(8,128)}, u32[]{:S(2)}) copy-start(f32[16,1024]{1,0:T(8,128)} %copy-done.6) | copy-start | bytes 196612
  229.3 17.6 %copy-start.5 = (f32[16,1024]{1,0:T(8,128)S(1)}, f32[16,1024]{1,0:T(8,128)}, u32[]{:S(2)}) copy-start(f32[16,1024]{1,0:T(8,128)} %copy-done.4) | copy-start | bytes 196612
  229.4 17.7 %copy-start.3 = (f32[16,1024]{1,0:T(8,128)S(1)}, f32[16,1024]{1,0:T(8,128)}, u32[]{:S(2)}) copy-start(f32[16,1024]{1,0:T(8,128)} %copy-done.2) | copy-start | bytes 196612
  247.1 1.4 copy-start.1
Sparse Core Ops, SparseCore 0:
  23.8 81.4 reduce-scatter.2
  262.8 6.7 reduce-scatter.4
